TPU v7x, 32 devices: a whole 2x2x4 slice. The times are simulated.
32 devices in a mesh: dp: 8 (over z, x), sp: 4 (over y, core).
Axes of the slice: x: 2, y: 2, z: 4, core: 2. Of those that a mesh axis runs over, the one named last changes fastest.
Arguments:
- inputs: bfloat16 [16, 512, 768], P('dp', 'sp'), may hold values from -6 to 6
- cotangent: bfloat16 [16, 512, 768], P('dp', 'sp'), may hold values from -6 to 6
- joined_weight: bfloat16 [768, 2304], P(('dp', 'sp')), may hold values from -0.21875 to 0.21875
- joined_bias: bfloat16 [2304], P(('dp', 'sp')), may hold values from -3 to 3
- dense_weight: bfloat16 [768, 768], P(('dp', 'sp')), may hold values from -1.75 to 1.75
- dense_bias: bfloat16 [768], P(('dp', 'sp')), may hold values from -3 to 3
- expand_weight: bfloat16 [768, 3072], P(('dp', 'sp')), may hold values from -0.21875 to 0.21875
- expand_bias: bfloat16 [3072], P(('dp', 'sp')), may hold values from -3 to 3
- shrink_weight: bfloat16 [3072, 768], P(('dp', 'sp')), may hold values from -0.109375 to 0.109375
- shrink_bias: bfloat16 [768], P(('dp', 'sp')), may hold values from -3 to 3
- attn_gain: bfloat16 [768], P(('dp', 'sp')), may hold values from 0.5 to 1.5
- attn_shift: bfloat16 [768], P(('dp', 'sp')), may hold values from -3 to 3
- mlp_gain: bfloat16 [768], P(('dp', 'sp')), may hold values from 0.5 to 1.5
- mlp_shift: bfloat16 [768], P(('dp', 'sp')), may hold values from -3 to 3
Outputs:
- output: bfloat16 [16, 512, 768], P('dp', 'sp')
- input_grad: float32 [16, 512, 768], P('dp', 'sp')
- joined_weight_grad: float32 [768, 2304], P(('dp', 'sp'))
- joined_bias_grad: float32 [2304], P(('dp', 'sp'))
- dense_weight_grad: float32 [768, 768], P(('dp', 'sp'))
- dense_bias_grad: float32 [768], P(('dp', 'sp'))
- expand_weight_grad: float32 [768, 3072], P(('dp', 'sp'))
- expand_bias_grad: float32 [3072], P(('dp', 'sp'))
- shrink_weight_grad: float32 [3072, 768], P(('dp', 'sp'))
- shrink_bias_grad: float32 [768], P(('dp', 'sp'))
- attn_gain_grad: float32 [768], P(('dp', 'sp'))
- attn_shift_grad: float32 [768], P(('dp', 'sp'))
- mlp_gain_grad: float32 [768], P(('dp', 'sp'))
- mlp_shift_grad: float32 [768], P(('dp', 'sp'))
All inputs are finite; a program needn't handle non-finite values.
Results may differ from a plain program's by a relative error of at most 0.011.
Values may be sent and summed in bfloat16 or wider, within the bound.
No kernel may reach another device: no remote copies, remote signals or barrier semaphores. Data moves between devices by JAX's collectives and lax.ppermute only.
A program may use at most 128 MiB of HBM per device.

v0:
```python
import jax
import jax.numpy as jnp
from jax import lax
from jax.sharding import PartitionSpec as P

HEADS = 12
HD = 64
ROT = 16


norm_eps = 1e-05


def layer_norm(values, gain, shift):
    mean_val = jnp.mean(values, axis=-1, keepdims=True)
    centred = values - mean_val
    variance = jnp.mean(centred * centred, axis=-1, keepdims=True)
    inv_std = lax.rsqrt(variance + norm_eps)
    normed = centred * inv_std
    return (normed, inv_std, normed * gain.astype(jnp.float32) + shift.astype(jnp.float32))


def norm_back(grad_out, normed, inv_std, gain):
    scaled = grad_out * gain.astype(jnp.float32)
    first = jnp.mean(scaled, axis=-1, keepdims=True)
    second = jnp.mean(scaled * normed, axis=-1, keepdims=True)
    return inv_std * (scaled - first - normed * second)


def rotary_tables(positions, rot_dims):
    freq = 1.0 / 10000.0 ** (jnp.arange(0, rot_dims, 2, dtype=jnp.float32) / rot_dims)
    angles = positions.astype(jnp.float32)[:, None] * freq[None, :]
    angles = jnp.concatenate([angles, angles], axis=-1)
    return (jnp.cos(angles), jnp.sin(angles))


def turn_half(part):
    half = part.shape[-1] // 2
    return jnp.concatenate([-part[..., half:], part[..., :half]], axis=-1)


def turn_half_back(part):
    half = part.shape[-1] // 2
    return jnp.concatenate([part[..., half:], -part[..., :half]], axis=-1)


def rotate_fwd(vec, cos_val, sin_val):
    rot_dims = cos_val.shape[-1]
    head_part = vec[..., :rot_dims]
    turned = head_part * cos_val + turn_half(head_part) * sin_val
    return jnp.concatenate([turned, vec[..., rot_dims:]], axis=-1)


def rotate_back(grad, cos_val, sin_val):
    rot_dims = cos_val.shape[-1]
    head_part = grad[..., :rot_dims]
    turned = head_part * cos_val + turn_half_back(head_part * sin_val)
    return jnp.concatenate([turned, grad[..., rot_dims:]], axis=-1)


def gelu_cdf(pre):
    return 0.5 * (1.0 + jax.scipy.special.erf(pre * 0.7071067811865476))


def gelu_slope(pre):
    return gelu_cdf(pre) + pre * jnp.exp(-0.5 * pre * pre) * 0.3989422804014327


def on_device(
    inputs,
    cotangent,
    joined_weight,
    joined_bias,
    dense_weight,
    dense_bias,
    expand_weight,
    expand_bias,
    shrink_weight,
    shrink_bias,
    attn_gain,
    attn_shift,
    mlp_gain,
    mlp_shift,
):
    gathered = (
        lax.all_gather(joined_weight, ("dp", "sp"), axis=0, tiled=True),
        lax.all_gather(joined_bias, ("dp", "sp"), axis=0, tiled=True),
        lax.all_gather(dense_weight, ("dp", "sp"), axis=0, tiled=True),
        lax.all_gather(dense_bias, ("dp", "sp"), axis=0, tiled=True),
        lax.all_gather(expand_weight, ("dp", "sp"), axis=0, tiled=True),
        lax.all_gather(expand_bias, ("dp", "sp"), axis=0, tiled=True),
        lax.all_gather(shrink_weight, ("dp", "sp"), axis=0, tiled=True),
        lax.all_gather(shrink_bias, ("dp", "sp"), axis=0, tiled=True),
        lax.all_gather(attn_gain, ("dp", "sp"), axis=0, tiled=True),
        lax.all_gather(attn_shift, ("dp", "sp"), axis=0, tiled=True),
        lax.all_gather(mlp_gain, ("dp", "sp"), axis=0, tiled=True),
        lax.all_gather(mlp_shift, ("dp", "sp"), axis=0, tiled=True),
    )
    (
        joined_full,
        joined_add,
        dense_full,
        dense_add,
        expand_full,
        expand_add,
        shrink_full,
        shrink_add,
        gain_a,
        shift_a,
        gain_b,
        shift_b,
    ) = gathered
    seq_count, local_len, width = inputs.shape
    token_count = seq_count * local_len
    sp_count = lax.axis_size("sp")
    full_len = local_len * sp_count
    head_group = HEADS // sp_count
    scale = HD ** (-0.5)
    block = min(512, full_len)
    block_count = full_len // block
    rows = inputs.reshape(token_count, width).astype(jnp.float32)
    normed, inv_std, affine_a = layer_norm(rows, gain_a, shift_a)
    affine_b = normed * gain_b.astype(jnp.float32) + shift_b.astype(jnp.float32)
    hidden_a = affine_a.astype(jnp.bfloat16)
    hidden_b = affine_b.astype(jnp.bfloat16)
    local_pos = lax.axis_index("sp") * local_len + jnp.arange(local_len, dtype=jnp.int32)
    cos_local, sin_local = rotary_tables(local_pos, ROT)
    cos_local = cos_local[None, :, None, :]
    sin_local = sin_local[None, :, None, :]
    joined = jnp.dot(hidden_a, joined_full, preferred_element_type=jnp.float32) + joined_add.astype(
        jnp.float32
    )
    joined = joined.reshape(seq_count, local_len, HEADS, 3, HD)
    query_rot = rotate_fwd(joined[:, :, :, 0], cos_local, sin_local)
    key_rot = rotate_fwd(joined[:, :, :, 1], cos_local, sin_local)
    rotated = (
        jnp.stack([query_rot, key_rot, joined[:, :, :, 2]], axis=3)
        .astype(jnp.bfloat16)
        .reshape(seq_count, local_len, 3 * width)
    )
    by_heads = lax.all_to_all(rotated, "sp", split_axis=2, concat_axis=1, tiled=True).reshape(
        seq_count, full_len, head_group, 3, HD
    )
    key_heads = by_heads[:, :, :, 1]
    value_heads = by_heads[:, :, :, 2]
    query_blocks = by_heads[:, :, :, 0]
    key_pos = jnp.arange(full_len, dtype=jnp.int32)
    row_pos = jnp.arange(block, dtype=jnp.int32)
    block_ids = jnp.arange(seq_count * block_count, dtype=jnp.int32)

    def block_scores(index):
        seq_id = index // block_count
        start = index % block_count * block
        query_blk = lax.dynamic_index_in_dim(query_blocks, index, 0, keepdims=False)
        keys = lax.dynamic_index_in_dim(key_heads, seq_id, 0, keepdims=False)
        values = lax.dynamic_index_in_dim(value_heads, seq_id, 0, keepdims=False)
        scores = (
            jnp.einsum("qhd,khd->hqk", query_blk, keys, preferred_element_type=jnp.float32) * scale
        )
        allowed = (start + row_pos)[:, None] >= key_pos[None, :]
        return (seq_id, query_blk, keys, values, scores, allowed)

    def attend(index):
        seq_id, query_blk, keys, values, scores, allowed = block_scores(index)
        log_total = jnp.log(jnp.sum(jnp.where(allowed, jnp.exp(scores), 0.0), axis=-1))
        weights = jnp.where(allowed, jnp.exp(scores - log_total[:, :, None]), 0.0).astype(
            jnp.bfloat16
        )
        context = jnp.einsum("hqk,khd->qhd", weights, values, preferred_element_type=jnp.float32)
        return (context, log_total)

    context_blocks, log_totals = lax.map(attend, block_ids)
    context_heads = context_blocks.astype(jnp.bfloat16).reshape(
        seq_count, full_len, head_group * HD
    )
    context_tokens = lax.all_to_all(
        context_heads, "sp", split_axis=1, concat_axis=2, tiled=True
    ).reshape(token_count, width)
    attn_out = jnp.dot(
        context_tokens, dense_full, preferred_element_type=jnp.float32
    ) + dense_add.astype(jnp.float32)
    pre = jnp.dot(hidden_b, expand_full, preferred_element_type=jnp.float32) + expand_add.astype(
        jnp.float32
    )
    activated = (pre * gelu_cdf(pre)).astype(jnp.bfloat16)
    mlp_out = jnp.dot(
        activated, shrink_full, preferred_element_type=jnp.float32
    ) + shrink_add.astype(jnp.float32)
    output = (rows + attn_out + mlp_out).astype(jnp.bfloat16).reshape(seq_count, local_len, width)
    joined_back, dense_back, expand_back, shrink_back, gain_a_back, gain_b_back = (
        joined_full,
        dense_full,
        expand_full,
        shrink_full,
        gain_a,
        gain_b,
    )
    cot_rows = cotangent.reshape(token_count, width)
    cot_f = cot_rows.astype(jnp.float32)
    out_bias_grad = jnp.sum(cot_f, axis=0)
    shrink_w_grad = jnp.einsum("tf,td->fd", activated, cot_rows, preferred_element_type=jnp.float32)
    act_grad = jnp.einsum("td,fd->tf", cot_rows, shrink_back, preferred_element_type=jnp.float32)
    pre_grad = act_grad * gelu_slope(pre)
    expand_b_grad = jnp.sum(pre_grad, axis=0)
    pre_grad_bf = pre_grad.astype(jnp.bfloat16)
    expand_w_grad = jnp.einsum(
        "td,tf->df", hidden_b, pre_grad_bf, preferred_element_type=jnp.float32
    )
    hidden_b_grad = jnp.einsum(
        "tf,df->td", pre_grad_bf, expand_back, preferred_element_type=jnp.float32
    )
    dense_w_grad = jnp.einsum(
        "td,te->de", context_tokens, cot_rows, preferred_element_type=jnp.float32
    )
    context_grad = jnp.einsum(
        "te,de->td", cot_rows, dense_back, preferred_element_type=jnp.float32
    ).astype(jnp.bfloat16)
    context_grad = context_grad.reshape(seq_count, local_len, width)
    grad_heads = lax.all_to_all(
        context_grad, "sp", split_axis=2, concat_axis=1, tiled=True
    ).reshape(seq_count * block_count, block, head_group, HD)

    def attend_back(carry, index):
        key_acc, value_acc = carry
        seq_id, query_blk, keys, values, scores, allowed = block_scores(index)
        log_total = lax.dynamic_index_in_dim(log_totals, index, 0, keepdims=False)
        probs = jnp.where(allowed, jnp.exp(scores - log_total[:, :, None]), 0.0)
        weights = probs.astype(jnp.bfloat16)
        grad_blk = lax.dynamic_index_in_dim(grad_heads, index, 0, keepdims=False)
        context_blk = lax.dynamic_index_in_dim(context_blocks, index, 0, keepdims=False)
        delta = jnp.sum(grad_blk.astype(jnp.float32) * context_blk, axis=-1)
        value_part = jnp.einsum(
            "hqk,qhd->khd", weights, grad_blk, preferred_element_type=jnp.float32
        )
        weight_grad = jnp.einsum(
            "qhd,khd->hqk", grad_blk, values, preferred_element_type=jnp.float32
        )
        score_grad = (probs * (weight_grad - delta.T[:, :, None]) * scale).astype(jnp.bfloat16)
        query_part = jnp.einsum(
            "hqk,khd->qhd", score_grad, keys, preferred_element_type=jnp.float32
        )
        key_part = jnp.einsum(
            "hqk,qhd->khd", score_grad, query_blk, preferred_element_type=jnp.float32
        )
        key_acc = key_acc.at[seq_id].add(key_part)
        value_acc = value_acc.at[seq_id].add(value_part)
        return ((key_acc, value_acc), query_part)

    empty_grad = jnp.zeros((seq_count, full_len, head_group, HD), jnp.float32)
    (key_grad, value_grad), query_grad = lax.scan(attend_back, (empty_grad, empty_grad), block_ids)
    cos_full, sin_full = rotary_tables(key_pos, ROT)
    cos_full = cos_full[None, :, None, :]
    sin_full = sin_full[None, :, None, :]
    joined_grad_heads = jnp.stack(
        [
            rotate_back(query_grad, cos_full, sin_full),
            rotate_back(key_grad, cos_full, sin_full),
            value_grad,
        ],
        axis=3,
    )
    joined_grad_heads = joined_grad_heads.astype(jnp.bfloat16).reshape(
        seq_count, full_len, head_group * 3 * HD
    )
    joined_grad = lax.all_to_all(
        joined_grad_heads, "sp", split_axis=1, concat_axis=2, tiled=True
    ).reshape(token_count, 3 * width)
    joined_b_grad = jnp.sum(joined_grad.astype(jnp.float32), axis=0)
    joined_w_grad = jnp.einsum(
        "td,tc->dc", hidden_a, joined_grad, preferred_element_type=jnp.float32
    )
    hidden_a_grad = jnp.einsum(
        "tc,dc->td", joined_grad, joined_back, preferred_element_type=jnp.float32
    )
    gain_a_grad = jnp.sum(hidden_a_grad * normed, axis=0)
    shift_a_grad = jnp.sum(hidden_a_grad, axis=0)
    gain_b_grad = jnp.sum(hidden_b_grad * normed, axis=0)
    shift_b_grad = jnp.sum(hidden_b_grad, axis=0)
    input_grad = (
        cot_f
        + norm_back(hidden_a_grad, normed, inv_std, gain_a_back)
        + norm_back(hidden_b_grad, normed, inv_std, gain_b_back)
    )
    input_grad = input_grad.reshape(seq_count, local_len, width)
    totals = (
        lax.psum_scatter(joined_w_grad, ("dp", "sp"), scatter_dimension=0, tiled=True),
        lax.psum_scatter(joined_b_grad, ("dp", "sp"), scatter_dimension=0, tiled=True),
        lax.psum_scatter(dense_w_grad, ("dp", "sp"), scatter_dimension=0, tiled=True),
        lax.psum_scatter(out_bias_grad, ("dp", "sp"), scatter_dimension=0, tiled=True),
        lax.psum_scatter(expand_w_grad, ("dp", "sp"), scatter_dimension=0, tiled=True),
        lax.psum_scatter(expand_b_grad, ("dp", "sp"), scatter_dimension=0, tiled=True),
        lax.psum_scatter(shrink_w_grad, ("dp", "sp"), scatter_dimension=0, tiled=True),
        lax.psum_scatter(out_bias_grad, ("dp", "sp"), scatter_dimension=0, tiled=True),
        lax.psum_scatter(gain_a_grad, ("dp", "sp"), scatter_dimension=0, tiled=True),
        lax.psum_scatter(shift_a_grad, ("dp", "sp"), scatter_dimension=0, tiled=True),
        lax.psum_scatter(gain_b_grad, ("dp", "sp"), scatter_dimension=0, tiled=True),
        lax.psum_scatter(shift_b_grad, ("dp", "sp"), scatter_dimension=0, tiled=True),
    )
    return (
        output,
        input_grad,
        totals[0],
        totals[1],
        totals[2],
        totals[3],
        totals[4],
        totals[5],
        totals[6],
        totals[7],
        totals[8],
        totals[9],
        totals[10],
        totals[11],
    )


def solution(mesh):
    in_specs = (
        P("dp", "sp", None),
        P("dp", "sp", None),
        P(("dp", "sp"), None),
        P(("dp", "sp")),
        P(("dp", "sp"), None),
        P(("dp", "sp")),
        P(("dp", "sp"), None),
        P(("dp", "sp")),
        P(("dp", "sp"), None),
        P(("dp", "sp")),
        P(("dp", "sp")),
        P(("dp", "sp")),
        P(("dp", "sp")),
        P(("dp", "sp")),
    )
    out_specs = (
        P("dp", "sp", None),
        P("dp", "sp", None),
        P(("dp", "sp"), None),
        P(("dp", "sp")),
        P(("dp", "sp"), None),
        P(("dp", "sp")),
        P(("dp", "sp"), None),
        P(("dp", "sp")),
        P(("dp", "sp"), None),
        P(("dp", "sp")),
        P(("dp", "sp")),
        P(("dp", "sp")),
        P(("dp", "sp")),
        P(("dp", "sp")),
    )
    return jax.shard_map(
        on_device, mesh=mesh, in_specs=in_specs, out_specs=out_specs, check_vma=False
    )
```

profile of v0, /device:TPU:0, one launch (start us, length us, event | category | flops | bytes accessed | tf_op | source)
XLA Modules:
  0.0 780.4 jit_solution(17766417555878121452)
XLA Ops:
  16.7 42.6 %all-reduce.16 = (bf16[768]{0:T(1024)(128)(2,1)S(1)}, bf16[768]{0:T(1024)(128)(2,1)S(1)}, bf16[3072]{0:T(1024)(128)(2,1)}, bf16[768]{0:T(1024)(128)(2,1)}, bf16[...) all-reduce(bf16[768]{0:T(1024)(128)(2,1)S(1)} %dynamic-update-slice, ...), channel_id=1, replica_groups=mesh['dp'=8,'sp'=4] {'dp','sp'}, use_global_device_ids=true, to_apply=%add.5 | all-reduce | flops 9984 | bytes 39936
  60.0 1.1 convert_reduce_fusion.2
  61.2 1.2 multiply_reduce_fusion.4
  63.0 2.0 add_convert_fusion.2
  65.0 8.8 %all-gather.5.cloned.1.call-done = bf16[768,2304]{1,0:T(8,128)(2,1)} async-done(((bf16[24,2304]{1,0:T(8,128)(2,1)}), bf16[768,2304]{1,0:T(8,128)(2,1)}) %all-gather.5.cloned.1.call-update) | async-done | bytes 3538960 | tf_op jit(solution)/shard_map/all_gather | solution.py:86
  73.8 4.5 convolution_add_fusion
  78.3 2.0 copy.74
  80.4 2.3 reshape.405
  82.6 1.4 slice.213
  84.1 1.5 slice_bitcast_fusion.1
  87.4 2.7 pad_maximum_fusion
  90.1 3.5 all-to-all-start
  94.3 35.3 %all-gather.7.cloned.1.call-done = bf16[768,768]{1,0:T(8,128)(2,1)} async-done(((bf16[24,768]{1,0:T(8,128)(2,1)}), bf16[768,768]{1,0:T(8,128)(2,1)}) %all-gather.7.cloned.1.call-update) | async-done | bytes 1179664 | tf_op jit(solution)/shard_map/all_gather | solution.py:88
  129.6 1.8 convolution_convert_fusion
  131.4 1.1 copy.86
  132.5 4.4 all-to-all-start.2
  138.6 9.0 %while.40 = (s32[]{:T(128)}, f32[2,512,3,64]{1,3,2,0:T(8,128)S(1)}, f32[2,3,512]{2,1,0:T(4,128)S(1)}, s32[2]{0:T(128)S(1)}, bf16[2,512,3,64]{1,3,2,0:T(8,128)(2,...) while((s32[]{:T(128)}, f32[2,512,3,64]{1,3,2,0:T(8,128)S(1)}, ...), condition=%wide.region_4.5_spmd.clone.clone, body=%wide.region_2.4_spmd.clone.clone.sunk | while | flops 207092224 | bytes 8105119 | solution.py:172
  141.3 1.0 select_reduce_fusion.2
  145.7 1.0 select_reduce_fusion.2
  147.7 1.1 copy.83
  148.8 3.5 all-to-all-start.1
  153.1 1.0 copy.87
  154.6 8.5 %all-to-all-done.1 = bf16[2,512,192]{2,0,1:T(2,128)(2,1)S(1)} async-done(((bf16[2,512,192]{2,0,1:T(2,128)(2,1)}), bf16[2,512,192]{2,0,1:T(2,128)(2,1)S(1)}, u32[]{:S(2)}, u32[]{:S(2)}) %all-to-all-start.1) | async-done | bytes 393248 | tf_op jit(solution)/shard_map/all_to_all | solution.py:176
  163.2 1.0 copy.95
  164.6 1.8 fusion.80
  167.0 1.0 broadcast.235.clone.1
  168.0 1.0 broadcast.235.clone.2
  169.0 22.5 %while.39 = (s32[]{:T(128)}, f32[2,512,3,64]{1,3,2,0:T(8,128)S(1)}, f32[2,512,3,64]{1,3,2,0:T(8,128)}, f32[2,512,3,64]{1,3,2,0:T(8,128)}, s32[2]{0:T(128)}, /*in...) while((s32[]{:T(128)}, f32[2,512,3,64]{1,3,2,0:T(8,128)S(1)}, ...), condition=%wide.region_8.9_spmd.clone, body=%wide.region_5.8_spmd.clone.sunk | while | flops 512916000 | bytes 25214336 | solution.py:250
  169.0 1.2 dynamic_slice.179
  173.0 1.5 multiply_convert_fusion.3
  176.0 1.0 fusion.152
  177.0 3.3 fusion.153
  180.3 1.2 dynamic_slice.179
  184.3 1.5 multiply_convert_fusion.3
  187.2 1.0 fusion.152
  188.3 3.3 fusion.153
  191.6 1.1 slice.215
  192.7 1.0 slice_multiply_fusion.3
  193.8 1.0 fusion.89
  194.9 1.2 convert_bitcast_fusion
  196.2 2.8 copy.89
  199.1 3.5 all-to-all-start.3
  202.7 1.0 add_convert_fusion
  203.7 17.2 %all-to-all-done.3 = bf16[2,512,576]{2,0,1:T(2,128)(2,1)S(1)} async-done(((bf16[2,512,576]{2,0,1:T(2,128)(2,1)}), bf16[2,512,576]{2,0,1:T(2,128)(2,1)S(1)}, u32[]{:S(2)}, u32[]{:S(2)}) %all-to-all-start.3) | async-done | bytes 1179680 | tf_op jit(solution)/shard_map/all_to_all | solution.py:265
  220.9 3.9 copy.90
  224.7 5.1 fusion.69
  230.5 5.9 multiply_convert_fusion.1
  236.4 24.1 %all-gather.11.cloned.1.call-done = bf16[3072,768]{1,0:T(8,128)(2,1)} async-done(((bf16[96,768]{1,0:T(8,128)(2,1)}), bf16[3072,768]{1,0:T(8,128)(2,1)}) %all-gather.11.cloned.1.call-update) | async-done | bytes 4718608 | tf_op jit(solution)/shard_map/all_gather | solution.py:92
  260.5 6.9 fusion.99
  267.4 1.2 copy-done.8
  268.6 5.1 fusion.76
  273.7 8.8 %reduce-scatter.11.cloned.1.call-start = ((), (), s32[]{:S(2)}) async-start(), calls=%async_computation.15 | async-start | bytes 9732096 | tf_op jit(solution)/shard_map/reduce_scatter | solution.py:292
  282.5 5.1 fusion.100
  290.1 5.3 convert_reduce_fusion
  296.1 4.5 fusion.78
  300.6 3.0 multiply_reduce_fusion.1
  303.7 41.1 %all-reduce.15 = (f32[2304]{0:T(1024)S(1)}, f32[768]{0:T(1024)S(1)}, f32[3072]{0:T(1024)S(1)}, f32[768]{0:T(1024)S(1)}, f32[768]{0:T(1024)S(1)}, /*index=5*/f32[768]{0:T(1024)S(1)}, f32[768]{0:T(1024)S(1)}) all-reduce(f32[2304]{0:T(1024)S(1)} %reduce_sum.154, ...), channel_id=3, replica_groups=mesh['dp'=8,'sp'=4] {'dp','sp'}, use_global_device_ids=true, to_apply=%region_15.16.clone | all-reduce | flops 9216 | bytes 73728
  351.0 3.8 convolution_add_fusion.3
  355.0 1.3 fusion.68
  356.3 1.4 multiply_add_fusion
  357.7 6.8 reduce-scatter.7.cloned.1.call-done
  364.5 124.7 %reduce-scatter.5.cloned.1.call-done = f32[24,2304]{1,0:T(8,128)} async-done(((f32[768,2304]{1,0:T(8,128)}), f32[24,2304]{1,0:T(8,128)}) %reduce-scatter.5.cloned.1.call-update) | async-done | bytes 221200 | tf_op jit(solution)/shard_map/reduce_scatter | solution.py:286
  489.1 141.8 %reduce-scatter.9.cloned.1.call-done = f32[24,3072]{1,0:T(8,128)} async-done(((f32[768,3072]{1,0:T(8,128)}), f32[24,3072]{1,0:T(8,128)}) %reduce-scatter.9.cloned.1.call-update) | async-done | bytes 294928 | tf_op jit(solution)/shard_map/reduce_scatter | solution.py:290
  631.0 141.8 %reduce-scatter.11.cloned.1.call-done = f32[96,768]{1,0:T(8,128)} async-done(((f32[3072,768]{1,0:T(8,128)}), f32[96,768]{1,0:T(8,128)}) %reduce-scatter.11.cloned.1.call-update) | async-done | bytes 294928 | tf_op jit(solution)/shard_map/reduce_scatter | solution.py:292
  (197 shorter events, 35.6 us)
Async XLA Ops:
  7.2 66.6 %all-gather.5.cloned.1.call-start = ((), (), s32[]{:S(2)}) async-start(), calls=%async_computation.8 | async-start | bytes 3649536 | tf_op jit(solution)/shard_map/all_gather | solution.py:86
  7.9 121.7 %all-gather.7.cloned.1.call-start = ((), (), s32[]{:S(2)}) async-start(), calls=%async_computation.9 | async-start | bytes 1216512 | tf_op jit(solution)/shard_map/all_gather | solution.py:88
  8.7 221.9 %all-gather.9.cloned.1.call-start = ((), (), s32[]{:S(2)}) async-start(), calls=%async_computation.10 | async-start | bytes 4866048 | tf_op jit(solution)/shard_map/all_gather | solution.py:90
  9.4 251.1 %all-gather.11.cloned.1.call-start = ((), (), s32[]{:S(2)}) async-start(), calls=%async_computation.11 | async-start | bytes 4866048 | tf_op jit(solution)/shard_map/all_gather | solution.py:92
  59.4 14.4 %copy-start.14 = (f32[768]{0:T(1024)}, f32[768]{0:T(1024)S(1)}, u32[]{:S(2)}) copy-start(f32[768]{0:T(1024)S(1)} %convert_element_type.134) | copy-start | bytes 9220
  59.4 14.4 %copy-start.16 = (f32[768]{0:T(1024)}, f32[768]{0:T(1024)S(1)}, u32[]{:S(2)}) copy-start(f32[768]{0:T(1024)S(1)} %convert_element_type.142) | copy-start | bytes 9220
  59.4 14.4 %copy-start.19 = (f32[768]{0:T(1024)}, f32[768]{0:T(1024)S(1)}, u32[]{:S(2)}) copy-start(f32[768]{0:T(1024)S(1)} %convert_element_type.135) | copy-start | bytes 9220
  59.4 0.5 copy-start.36
  61.1 1.8 copy-start.29
  61.1 12.6 %copy-start.23 = (f32[256]{0:T(256)}, f32[256]{0:T(256)S(1)}, u32[]{:S(2)}) copy-start(f32[256]{0:T(256)S(1)} %get-tuple-element.577) | copy-start | bytes 3076
  63.0 10.8 %copy-start.26 = (f32[256]{0:T(256)}, f32[256]{0:T(256)S(1)}, u32[]{:S(2)}) copy-start(f32[256]{0:T(256)S(1)} %get-tuple-element.576) | copy-start | bytes 3076
  86.4 43.2 %copy-start.1 = (bf16[2,128,768]{2,1,0:T(8,128)(2,1)S(1)}, bf16[2,128,768]{2,1,0:T(8,128)(2,1)}, u32[]{:S(2)}) copy-start(bf16[2,128,768]{2,1,0:T(8,128)(2,1)} %param.23) | copy-start | bytes 1179652
  90.1 42.3 %all-to-all-start = ((bf16[2,128,2304]{1,0,2:T(2,128)(2,1)}), bf16[2,128,2304]{1,0,2:T(2,128)(2,1)S(1)}, u32[]{:S(2)}, u32[]{:S(2)}) async-start(bf16[2,128,2304]{1,0,2:T(2,128)(2,1)} %bitcast.7), calls=%async_computation | async-start | bytes 2359296 | tf_op jit(solution)/shard_map/all_to_all | solution.py:141
  132.5 16.3 %all-to-all-start.2 = ((bf16[2,128,768]{1,0,2:T(2,128)(2,1)}), bf16[2,128,768]{1,0,2:T(2,128)(2,1)}, u32[]{:S(2)}, u32[]{:S(2)}) async-start(bf16[2,128,768]{1,0,2:T(2,128)(2,1)} %copy.86), calls=%async_computation.2 | async-start | bytes 786432 | tf_op jit(solution)/shard_map/all_to_all | solution.py:219
  147.6 1.2 copy-start.12
  147.6 4.7 copy-start.31
  147.6 4.7 copy-start.37
  148.8 14.4 %all-to-all-start.1 = ((bf16[2,512,192]{2,0,1:T(2,128)(2,1)}), bf16[2,512,192]{2,0,1:T(2,128)(2,1)S(1)}, u32[]{:S(2)}, u32[]{:S(2)}) async-start(bf16[2,512,192]{2,0,1:T(2,128)(2,1)} %copy.83), calls=%async_computation.1 | async-start | bytes 1048576 | tf_op jit(solution)/shard_map/all_to_all | solution.py:176
  152.3 212.2 %reduce-scatter.7.cloned.1.call-start = ((), (), s32[]{:S(2)}) async-start(), calls=%async_computation.13 | async-start | bytes 2433024 | tf_op jit(solution)/shard_map/reduce_scatter | solution.py:288
  164.5 1.9 copy-start.3
  166.4 2.6 copy-start.13
  173.0 1.5 copy-start.5
  173.0 2.1 copy-start.22
  175.2 1.8 copy-start.6
  184.3 1.6 copy-start.5
  184.3 2.2 copy-start.22
  186.4 1.8 copy-start.6
  196.2 6.5 copy-start
  196.2 6.5 copy-start.15
  196.2 6.5 copy-start.20
  196.2 6.5 copy-start.30
  196.2 6.5 copy-start.33
  199.1 21.8 %all-to-all-start.3 = ((bf16[2,512,576]{2,0,1:T(2,128)(2,1)}), bf16[2,512,576]{2,0,1:T(2,128)(2,1)S(1)}, u32[]{:S(2)}, u32[]{:S(2)}) async-start(bf16[2,512,576]{2,0,1:T(2,128)(2,1)} %copy.89), calls=%async_computation.3 | async-start | bytes 2621440 | tf_op jit(solution)/shard_map/all_to_all | solution.py:265
  202.6 286.5 %reduce-scatter.5.cloned.1.call-start = ((), (), s32[]{:S(2)}) async-start(), calls=%async_computation.12 | async-start | bytes 7299072 | tf_op jit(solution)/shard_map/reduce_scatter | solution.py:286
  229.8 0.7 copy-start.32
  229.8 401.1 %reduce-scatter.9.cloned.1.call-start = ((), (), s32[]{:S(2)}) async-start(), calls=%async_computation.14 | async-start | bytes 9732096 | tf_op jit(solution)/shard_map/reduce_scatter | solution.py:290
  260.5 8.1 %copy-start.7 = (bf16[256,768]{1,0:T(8,128)(2,1)S(1)}, bf16[256,768]{1,0:T(8,128)(2,1)}, u32[]{:S(2)}) copy-start(bf16[256,768]{1,0:T(8,128)(2,1)} %get-tuple-element.560) | copy-start | bytes 1179652
  267.4 1.2 copy-start.8
  273.7 499.1 %reduce-scatter.11.cloned.1.call-start = ((), (), s32[]{:S(2)}) async-start(), calls=%async_computation.15 | async-start | bytes 9732096 | tf_op jit(solution)/shard_map/reduce_scatter | solution.py:292
  287.5 0.7 copy-start.35
  287.5 1.3 copy-start.34
  296.1 4.5 copy-start.17
  296.1 4.5 copy-start.24
  296.1 4.5 copy-start.27
  296.1 4.5 copy-start.38
  300.6 3.0 copy-start.9
  344.9 428.0 %copy-start.39 = (f32[24]{0:T(128)}, f32[24]{0:T(128)S(1)}, u32[]{:S(2)}) copy-start(f32[24]{0:T(128)S(1)} %dynamic-slice.39) | copy-start | bytes 292
  351.0 3.9 copy-start.2
  351.0 3.9 copy-start.4
  351.0 3.9 copy-start.21
  354.9 1.4 copy-start.10
  354.9 1.4 copy-start.11
  354.9 1.4 copy-start.18
  354.9 1.4 copy-start.25
  354.9 1.4 copy-start.28
Sparse Core Ops, SparseCore 0:
  10.9 62.8 all-gather.4
  76.7 52.8 all-gather.6
  132.5 62.5 all-gather.8
  197.8 62.5 all-gather.10
  266.2 98.2 reduce-scatter.6
  370.6 118.5 reduce-scatter.4
  495.6 135.3 reduce-scatter.8
  637.5 135.3 reduce-scatter.10
where the time goes:
time: 789 us; the launch traced here: 780 us
  waiting for transfers between devices  512 us (65%)
  blocking collectives  83.8 us (11%)
  matrix products  66.5 us (8%)
  local copies, waits for them, and re-layouts  43.2 us (5%)
  other arithmetic  28.2 us (4%)
  starting transfers between devices  24 us (3%)
  between operations  15.1 us (2%)
  loops' own time  8.04 us (1%)
    reduce_scatter x1, waiting for transfers between devices, on_device(): lax.psum_scatter(shrink_w_grad, ('dp', 'sp'), scatter_dimension=0, tiled=...  142 us
    reduce_scatter x1, waiting for transfers between devices, on_device(): lax.psum_scatter(expand_w_grad, ('dp', 'sp'), scatter_dimension=0, tiled=...  142 us
    reduce_scatter x1, waiting for transfers between devices, on_device(): lax.psum_scatter(joined_w_grad, ('dp', 'sp'), scatter_dimension=0, tiled=...  125 us
    unnamed x2, blocking collectives  83.8 us
    all_gather x1, waiting for transfers between devices, on_device(): lax.all_gather(dense_weight, ('dp', 'sp'), axis=0, tiled=True)  35.3 us
    all_gather x1, waiting for transfers between devices, on_device(): lax.all_gather(shrink_weight, ('dp', 'sp'), axis=0, tiled=True)  24.1 us
    all_to_all x1, waiting for transfers between devices, on_device(): lax.all_to_all(joined_grad_heads, 'sp', split_axis=1, concat_axis=2, tile...  17.2 us
  transfers between devices with their start and end apart: 12, of which 9 were waited for; matrix products, arithmetic and copies ran while one was open for 17% of the time, Pallas kernels for 0%

commit v1 on v0

v1 whole, which is shorter than its diff:
```python
import jax
import jax.numpy as jnp
from jax import lax
from jax.sharding import PartitionSpec as P

HEADS = 12
HD = 64
ROT = 16
NORM_EPS = 1e-05
BF = jnp.bfloat16
F32 = jnp.float32


def bits_of(count):
    assert count & (count - 1) == 0
    bit = 1
    out = []
    while bit < count:
        out.append(bit)
        bit *= 2
    return out


def swap(value, axis, bit):
    count = lax.axis_size(axis)
    return lax.ppermute(value, axis, [(i, i ^ bit) for i in range(count)])


def cube_gather(value, axis):
    order = [0]
    for bit in reversed(bits_of(lax.axis_size(axis))):
        value = jnp.concatenate([value, swap(value, axis, bit)], axis=0)
        order = order + [k ^ bit for k in order]
    return value, order


def cube_scatter(value, axis, wire):
    for bit in bits_of(lax.axis_size(axis)):
        half = value.shape[0] // 2
        keep, send = value[:half], value[half:]
        got = swap(send.astype(wire), axis, bit)
        value = keep.astype(F32) + got.astype(F32)
    return value


def to_natural(blocks, order, axis):
    me = lax.axis_index(axis)
    inverse = [order.index(k) for k in range(len(order))]
    ids = jnp.asarray(inverse, jnp.int32)[jnp.arange(len(order), dtype=jnp.int32) ^ me]
    return blocks[ids]


def layer_norm(values):
    mean_val = jnp.mean(values, axis=-1, keepdims=True)
    centred = values - mean_val
    variance = jnp.mean(centred * centred, axis=-1, keepdims=True)
    inv_std = lax.rsqrt(variance + NORM_EPS)
    return centred * inv_std, inv_std


def rotary_tables(positions):
    freq = 1.0 / 10000.0 ** (jnp.arange(0, ROT, 2, dtype=F32) / ROT)
    angles = positions.astype(F32)[:, None] * freq[None, :]
    angles = jnp.concatenate([angles, angles], axis=-1)
    return jnp.cos(angles), jnp.sin(angles)


def turn_half(part):
    half = part.shape[-1] // 2
    return jnp.concatenate([-part[..., half:], part[..., :half]], axis=-1)


def turn_half_back(part):
    half = part.shape[-1] // 2
    return jnp.concatenate([part[..., half:], -part[..., :half]], axis=-1)


def rotate_fwd(vec, cos_val, sin_val):
    head_part = vec[..., :ROT]
    turned = head_part * cos_val + turn_half(head_part) * sin_val
    return jnp.concatenate([turned, vec[..., ROT:]], axis=-1)


def rotate_back(grad, cos_val, sin_val):
    head_part = grad[..., :ROT]
    turned = head_part * cos_val + turn_half_back(head_part * sin_val)
    return jnp.concatenate([turned, grad[..., ROT:]], axis=-1)


def dot(left, right, dims):
    return lax.dot_general(left, right, (dims, ((), ())), preferred_element_type=F32)


def on_device(
    inputs,
    cotangent,
    joined_weight,
    joined_bias,
    dense_weight,
    dense_bias,
    expand_weight,
    expand_bias,
    shrink_weight,
    shrink_bias,
    attn_gain,
    attn_shift,
    mlp_gain,
    mlp_shift,
):
    seqs, local_len, width = inputs.shape
    sp, dp = lax.axis_size("sp"), lax.axis_size("dp")
    me = lax.axis_index("sp")
    heads = HEADS // sp
    local = seqs * local_len
    tokens = local * sp
    full_len = local_len * sp
    scale = HD ** (-0.5)
    cols = joined_weight.shape[1] // sp
    row_n = joined_weight.shape[0]
    ff_n = shrink_weight.shape[0]
    ff_all = expand_weight.shape[1]
    units = ff_all // sp

    small_parts = (
        joined_bias,
        dense_bias,
        expand_bias,
        shrink_bias,
        attn_gain,
        attn_shift,
        mlp_gain,
        mlp_shift,
    )
    sizes = [part.shape[0] for part in small_parts]
    offsets = [sum(sizes[:i]) for i in range(len(sizes))]
    small = jnp.concatenate(small_parts)[None, :]
    small, order = cube_gather(small, "sp")
    small = to_natural(small, order, "sp")[None]
    small, dp_order = cube_gather(small, "dp")
    small = to_natural(small, dp_order, "dp").astype(F32)

    def whole(index):
        return small[:, :, offsets[index] : offsets[index] + sizes[index]].reshape(-1)

    joined_add = lax.dynamic_slice_in_dim(whole(0), me * cols, cols)
    out_add = whole(1) + whole(3)
    expand_all = small[:, :, offsets[2] : offsets[2] + sizes[2]]
    expand_add = lax.dynamic_index_in_dim(expand_all, me, 1, keepdims=False).reshape(-1)
    gain_a, shift_a, gain_b, shift_b = whole(4), whole(5), whole(6), whole(7)

    expand_part = (
        expand_weight.reshape(row_n, dp, sp, ff_n).transpose(0, 2, 1, 3).reshape(row_n, ff_all)
    )
    expand_part = lax.all_to_all(expand_part, "sp", split_axis=1, concat_axis=0, tiled=True)
    joined_part = lax.all_to_all(joined_weight, "sp", split_axis=1, concat_axis=0, tiled=True)
    expand_w = lax.all_gather(expand_part, "dp", axis=0, tiled=True)
    shrink_w = lax.all_gather(shrink_weight, "dp", axis=0, tiled=True)
    joined_w = lax.all_gather(joined_part, "dp", axis=0, tiled=True)
    dense_rows = lax.all_gather(dense_weight, "dp", axis=0, tiled=True)
    dense_w = lax.all_to_all(dense_rows, "sp", split_axis=0, concat_axis=0, tiled=True)
    dense_w = dense_w.reshape(sp, dp // sp, row_n, width).transpose(1, 0, 2, 3)
    dense_w = dense_w.reshape(heads * HD, width)

    x_bf, order = cube_gather(inputs.reshape(1, local, width), "sp")
    cot_bf, _ = cube_gather(cotangent.reshape(1, local, width), "sp")
    x_bf = x_bf.reshape(tokens, width)
    cot_bf = cot_bf.reshape(tokens, width)
    normed, _ = layer_norm(x_bf.astype(F32))
    hidden_a = (normed * gain_a + shift_a).astype(BF)
    hidden_b = (normed * gain_b + shift_b).astype(BF)
    starts = jnp.asarray(order, jnp.int32) ^ me
    pos = (starts[:, None] * local_len + jnp.arange(local_len, dtype=jnp.int32)).reshape(-1)

    pre = dot(hidden_b, expand_w, ((1,), (0,))) + expand_add
    cdf = 0.5 * (1.0 + lax.erf(pre * 0.7071067811865476))
    activated = (pre * cdf).astype(BF)
    slope = cdf + pre * jnp.exp(-0.5 * pre * pre) * 0.3989422804014327
    act_grad = dot(cot_bf, shrink_w, ((1,), (1,)))
    pre_grad = act_grad * slope
    pre_grad_bf = pre_grad.astype(BF)
    expand_b_grad = jnp.sum(pre_grad, axis=0)
    expand_w_grad = dot(hidden_b, pre_grad_bf, ((0,), (0,)))
    shrink_w_grad = dot(activated, cot_bf, ((0,), (0,)))
    mlp_part = dot(activated, shrink_w, ((1,), (0,)))
    hidden_b_grad = dot(pre_grad_bf, expand_w, ((1,), (1,)))

    cos_val, sin_val = rotary_tables(pos)
    cos_val, sin_val = cos_val[:, None, None, :], sin_val[:, None, None, :]

    def by_seq(value):
        value = value.reshape(sp, seqs, local_len, value.shape[-1])
        return value.transpose(1, 0, 2, 3).reshape(seqs, full_len, -1)

    def by_block(value):
        value = value.reshape(seqs, sp, local_len, value.shape[-1])
        return value.transpose(1, 0, 2, 3).reshape(tokens, -1)

    joined = dot(by_seq(hidden_a).reshape(tokens, width), joined_w, ((1,), (0,))) + joined_add
    joined = joined.reshape(seqs, full_len, heads, 3, HD)
    cos_val = cos_val.reshape(1, full_len, 1, ROT)
    sin_val = sin_val.reshape(1, full_len, 1, ROT)
    query = rotate_fwd(joined[:, :, :, 0], cos_val, sin_val).astype(BF)
    key = rotate_fwd(joined[:, :, :, 1], cos_val, sin_val).astype(BF)
    value = joined[:, :, :, 2].astype(BF)
    scores = jnp.einsum("bqhd,bkhd->bhqk", query, key, preferred_element_type=F32) * scale
    allowed = (pos[:, None] >= pos[None, :])[None, None]
    log_total = jnp.log(
        jnp.sum(jnp.where(allowed, jnp.exp(scores), 0.0), axis=-1, keepdims=True)
    )
    probs = jnp.where(allowed, jnp.exp(scores - log_total), 0.0)
    weights = probs.astype(BF)
    context = jnp.einsum("bhqk,bkhd->bqhd", weights, value, preferred_element_type=F32)
    context_bf = by_block(context.astype(BF).reshape(seqs, full_len, heads * HD))
    attn_part = dot(context_bf, dense_w, ((1,), (0,)))
    dense_w_grad = dot(context_bf, cot_bf, ((0,), (0,)))
    context_grad = dot(cot_bf, dense_w, ((1,), (1,))).astype(BF)
    context_grad = by_seq(context_grad).reshape(seqs, full_len, heads, HD)
    delta = jnp.sum(context_grad.astype(F32) * context, axis=-1).transpose(0, 2, 1)[..., None]
    value_grad = jnp.einsum("bhqk,bqhd->bkhd", weights, context_grad, preferred_element_type=F32)
    weight_grad = jnp.einsum("bqhd,bkhd->bhqk", context_grad, value, preferred_element_type=F32)
    score_grad = (probs * (weight_grad - delta) * scale).astype(BF)
    query_grad = jnp.einsum("bhqk,bkhd->bqhd", score_grad, key, preferred_element_type=F32)
    key_grad = jnp.einsum("bhqk,bqhd->bkhd", score_grad, query, preferred_element_type=F32)
    joined_grad = jnp.stack(
        [
            rotate_back(query_grad, cos_val, sin_val),
            rotate_back(key_grad, cos_val, sin_val),
            value_grad,
        ],
        axis=3,
    ).astype(BF)
    joined_grad = by_block(joined_grad.reshape(seqs, full_len, cols))
    joined_b_grad = jnp.sum(joined_grad.astype(F32), axis=0)
    joined_w_grad = dot(hidden_a, joined_grad, ((0,), (0,)))
    hidden_a_grad = dot(joined_grad, joined_w, ((1,), (1,)))

    rows = inputs.reshape(local, width).astype(F32)
    out_sum = cube_scatter((attn_part + mlp_part).reshape(sp, local, width), "sp", BF)[0]
    output = (rows + out_sum + out_add).astype(BF).reshape(inputs.shape)
    scaled = (hidden_a_grad * gain_a + hidden_b_grad * gain_b).reshape(sp, local, width)
    scaled = cube_scatter(scaled, "sp", BF)[0]
    own_normed, own_inv = layer_norm(rows)
    first = jnp.mean(scaled, axis=-1, keepdims=True)
    second = jnp.mean(scaled * own_normed, axis=-1, keepdims=True)
    cot_f = cotangent.reshape(local, width).astype(F32)
    input_grad = cot_f + own_inv * (scaled - first - own_normed * second)
    input_grad = input_grad.reshape(inputs.shape)

    def reduce_rows(grad):
        return lax.psum_scatter(grad.astype(BF), "dp", scatter_dimension=0, tiled=True)

    expand_g = reduce_rows(expand_w_grad)
    expand_g = lax.all_to_all(expand_g, "sp", split_axis=0, concat_axis=1, tiled=True)
    expand_g = expand_g.reshape(row_n, sp, dp, ff_n).transpose(0, 2, 1, 3).reshape(row_n, ff_all)
    shrink_g = reduce_rows(shrink_w_grad)
    joined_g = reduce_rows(joined_w_grad)
    joined_g = lax.all_to_all(joined_g, "sp", split_axis=0, concat_axis=1, tiled=True)
    dense_g = dense_w_grad.astype(BF).reshape(dp // sp, sp, row_n, width).transpose(1, 0, 2, 3)
    dense_g = dense_g.reshape(heads * HD, width)
    dense_g = lax.all_to_all(dense_g, "sp", split_axis=0, concat_axis=0, tiled=True)
    dense_g = reduce_rows(dense_g)

    joined_b_all = lax.dynamic_update_slice_in_dim(
        jnp.zeros((cols * sp,), F32), joined_b_grad, me * cols, 0
    )
    mine = (jnp.arange(sp, dtype=jnp.int32) == me)[None, :, None]
    expand_b_all = jnp.where(mine, expand_b_grad.reshape(dp, 1, ff_n), 0.0)

    def split(vector):
        return vector.reshape(dp, sp, -1)

    small_grad = jnp.concatenate(
        [
            split(joined_b_all),
            expand_b_all,
            split(jnp.sum(cot_f, axis=0)),
            split(jnp.sum(hidden_a_grad * normed, axis=0)),
            split(jnp.sum(hidden_a_grad, axis=0)),
            split(jnp.sum(hidden_b_grad * normed, axis=0)),
            split(jnp.sum(hidden_b_grad, axis=0)),
        ],
        axis=2,
    )
    dp_me = lax.axis_index("dp")
    small_grad = small_grad[jnp.asarray(dp_order, jnp.int32) ^ dp_me]
    small_grad = cube_scatter(small_grad, "dp", F32)[0]
    small_grad = small_grad[jnp.asarray(order, jnp.int32) ^ me]
    small_grad = cube_scatter(small_grad, "sp", F32)[0]
    s_sizes = [sizes[0], sizes[2], sizes[1], sizes[4], sizes[5], sizes[6], sizes[7]]
    at = [sum(s_sizes[:i]) for i in range(len(s_sizes))]
    pieces = [small_grad[a : a + n] for a, n in zip(at, s_sizes)]
    joined_bg, expand_bg, out_bg, gain_ag, shift_ag, gain_bg, shift_bg = pieces
    return (
        output,
        input_grad,
        joined_g.astype(F32),
        joined_bg,
        dense_g.astype(F32),
        out_bg,
        expand_g.astype(F32),
        expand_bg,
        shrink_g.astype(F32),
        out_bg,
        gain_ag,
        shift_ag,
        gain_bg,
        shift_bg,
    )


def solution(mesh):
    token = P("dp", "sp", None)
    matrix = P(("dp", "sp"), None)
    vector = P(("dp", "sp"))
    params = (matrix, vector) * 4 + (vector,) * 4
    return jax.shard_map(
        on_device,
        mesh=mesh,
        in_specs=(token, token) + params,
        out_specs=(token, token) + params,
        check_vma=False,
    )
```

time: 789 us -> 476 us (0.60)
  waiting for transfers between devices: 512 us -> 205 us
  local copies, waits for them, and re-layouts: 43.2 us -> 58.6 us
  matrix products: 66.5 us -> 54.8 us
  loops' own time: 8.04 us -> 0 us
    reduce_scatter x4, waiting for transfers between devices: 415 us -> 163 us  [reduce_rows(): lax.psum_scatter(grad.astype(BF), 'dp', scatter_dimension=0, tiled=True)]
    unnamed x2 -> x0, blocking collectives: 83.8 us -> none
    all_gather x0 -> x2, blocking collectives: none -> 69.7 us  [the longest x1 35.8 us: on_device(): joined_w = lax.all_gather(joined_part, 'dp', axis=0, tiled=True)]
    all_gather x4 -> x2, waiting for transfers between devices: 68.2 us -> 0.02 us  [the longest x1 0.02 us: on_device(): expand_w = lax.all_gather(expand_part, 'dp', axis=0, tiled=True)]
    ppermute x0 -> x18, waiting for transfers between devices: none -> 33.3 us  [swap(): return lax.ppermute(value, axis, [(i, i ^ bit) for i in range(count)])]
    dot_general x26 -> x17, matrix products: 66.5 us -> 47.2 us  [the longest x12 39.7 us: dot(): lax.dot_general(left, right, (dims, ((), ())), preferred_element_type=F32)]
    all_to_all x4 -> x5, waiting for transfers between devices: 25.7 us -> 7.59 us  [the longest x1 5.16 us: on_device(): lax.all_to_all(dense_g, 'sp', split_axis=0, concat_axis=0, tiled=True)]
    ppermute x0 -> x18, starting transfers between devices: none -> 9.73 us  [swap(): return lax.ppermute(value, axis, [(i, i ^ bit) for i in range(count)])]
  transfers between devices with their start and end apart: 12 -> 29, of which waited for: 9 -> 14; matrix products, arithmetic and copies ran while one was open for 17% -> 28% of each run, Pallas kernels for 0% -> 0%
where the time goes in v1:
time: 476 us; the launch traced here: 469 us
  waiting for transfers between devices  205 us (43%)
  blocking collectives  78.7 us (17%)
  local copies, waits for them, and re-layouts  58.6 us (12%)
  matrix products  54.8 us (12%)
  other arithmetic  29.3 us (6%)
  starting transfers between devices  27.3 us (6%)
  between operations  15.6 us (3%)
    reduce_scatter x4, waiting for transfers between devices, reduce_rows(): lax.psum_scatter(grad.astype(BF), 'dp', scatter_dimension=0, tiled=True)  163 us
    dot_general x12, matrix products, dot(): lax.dot_general(left, right, (dims, ((), ())), preferred_element_type=F32)  39.7 us
    all_gather x1, blocking collectives, on_device(): joined_w = lax.all_gather(joined_part, 'dp', axis=0, tiled=True)  35.8 us
    all_gather x1, blocking collectives, on_device(): dense_rows = lax.all_gather(dense_weight, 'dp', axis=0, tiled=True)  33.9 us
    ppermute x18, waiting for transfers between devices, swap(): return lax.ppermute(value, axis, [(i, i ^ bit) for i in range(count)])  33.3 us
    ppermute x18, starting transfers between devices, swap(): return lax.ppermute(value, axis, [(i, i ^ bit) for i in range(count)])  9.73 us
  transfers between devices with their start and end apart: 29, of which 14 were waited for; matrix products, arithmetic and copies ran while one was open for 28% of the time, Pallas kernels for 0%

profile of v1, /device:TPU:0, one launch (start us, length us, event | category | flops | bytes accessed | tf_op | source)
XLA Modules:
  0.0 468.9 jit_solution(3307206197385059401)
XLA Ops:
  7.3 1.2 reshape.595
  8.6 8.9 %all_to_all.85 = bf16[24,4,768]{2,0,1:T(8,128)(2,1)} all-to-all(bf16[24,4,768]{2,0,1:T(8,128)(2,1)S(1)} %all_to_all.68), channel_id=1, replica_groups=mesh['dp'=8,'sp'=4] {'sp'}, dimensions={1} | all-to-all | bytes 294912 | tf_op jit(solution)/shard_map/all_to_all | solution.py:154
  18.1 5.4 %concatenate.92 = bf16[312]{0:T(512)(128)(2,1)S(1)} concatenate(bf16[72]{0:T(256)(128)(2,1)} %param.22, bf16[24]{0:T(256)(128)(2,1)} %param.24, bf16[96]{0:T(256)(128)(2,1)} %param.26, bf16[24]{0:T(256)(128)(2,1)} %param.28, bf16[24]{0:T(256)(128)(2,1)} %param.29, bf16[24]{0:T(256)(128)(2,1)} %param.30, bf16[24]{0:T(256)(128)(2,1)} %param.31, bf16[24]{0:T(256)(128)(2,1)} %param.32), dimensions={0} | concatenate | bytes 1248 | tf_op jit(solution)/shard_map/concatenate | solution.py:136
  23.5 1.7 collective-permute-start.2
  27.3 3.3 all-to-all-start
  33.5 33.9 %all_gather.13 = bf16[192,768]{1,0:T(8,128)(2,1)} all-gather(bf16[24,768]{1,0:T(8,128)(2,1)S(1)} %copy-done.22), channel_id=1, replica_groups=mesh['dp'=8,'sp'=4] {'dp'}, dimensions={0}, use_global_device_ids=true | all-gather | bytes 331776 | tf_op jit(solution)/shard_map/all_gather | solution.py:159
  70.7 1.1 collective-permute-done.3
  72.5 4.5 collective-permute-done.4
  77.7 3.0 collective-permute-done.5
  80.7 1.6 collective-permute-start.6
  82.8 1.7 collective-permute-done.6
  89.3 3.5 all-to-all-start.1
  92.8 35.8 %all_gather.12 = bf16[768,576]{1,0:T(8,128)(2,1)} all-gather(bf16[96,576]{1,0:T(8,128)(2,1)} %bitcast.227), channel_id=1, replica_groups=mesh['dp'=8,'sp'=4] {'dp'}, dimensions={0}, use_global_device_ids=true | all-gather | bytes 995328 | tf_op jit(solution)/shard_map/all_gather | solution.py:158
  134.4 2.6 convolution_add_fusion.1
  136.9 4.4 reshape.591
  141.3 1.9 fusion.72
  143.2 1.4 slice.274
  147.9 2.5 pad_maximum_fusion.1
  150.4 2.1 convolution_convert_fusion.3
  153.1 1.3 fusion.43
  154.3 7.6 %fusion.2 = f32[2,3,512,512]{2,3,1,0:T(8,128)} fusion(pred[512,512]{0,1:T(8,128)(4,1)} %broadcast_compare_fusion, bf16[2,512,3,48]{1,3,2,0:T(8,128)(2,1)} %slice.373, bf16[2,512,3,16]{1,3,2,0:T(8,128)(2,1)S(1)} %get-tuple-element.39, bf16[2,512,3,48]{1,3,2,0:T(8,128)(2,1)} %slice.374, bf16[2,512,3,16]{1,3,2,0:T(8,128)(2,1)S(1)} %get-tuple-element.38), kind=kOutput, calls=%fused_computation.9 | convolution fusion | flops 413666816 | bytes 7340032 | tf_op jit(solution)/shard_map/reduce_sum | solution.py:208
  162.0 3.6 multiply_reduce_fusion.3
  171.6 1.2 copy.93
  172.8 2.5 convert_element_type.190
  175.3 2.9 copy.94
  178.2 4.1 reshape.599
  182.4 1.4 copy.123
  183.7 1.3 reshape.592
  185.0 2.0 convolution_convert_fusion.4
  187.8 3.6 all-to-all-start.4
  191.4 1.6 add_convert_fusion
  193.0 5.2 %all-to-all-done.4 = bf16[4,48,768]{2,1,0:T(8,128)(2,1)S(1)} async-done(((bf16[4,48,768]{2,1,0:T(8,128)(2,1)}), bf16[4,48,768]{2,1,0:T(8,128)(2,1)S(1)}, u32[]{:S(2)}, u32[]{:S(2)}) %all-to-all-start.4) | async-done | bytes 294944 | tf_op jit(solution)/shard_map/all_to_all | solution.py:260
  198.9 4.2 convolution_convert_fusion.2
  203.1 4.6 fusion.78
  207.8 1.4 convert_reduce_fusion.1
  210.3 1.5 add_convert_fusion.1
  211.9 4.4 multiply_convert_fusion.1
  216.3 5.5 %fusion.76 = (f32[768]{0:T(1024)}, bf16[1024,768]{1,0:T(8,128)(2,1)S(1)}) fusion(f32[1024,768]{1,0:T(8,128)} %get-tuple-element.69, f32[768]{0:T(1024)S(1)} %copy-done.31, bf16[1024,768]{1,0:T(8,128)(2,1)} %bitcast.33, bf16[768,768]{1,0:T(8,128)(2,1)} %all-gather.5.cloned.1.call-done), kind=kOutput, calls=%fused_computation.188 | convolution fusion | flops 1217395968 | bytes 7477248 | tf_op jit(solution)/shard_map/dot_general | solution.py:91
  221.8 1.1 copy-done.41
  222.9 2.5 convolution_convert_fusion.1
  225.8 5.4 %fusion.69 = (f32[768]{0:T(1024)S(1)}, f32[768]{0:T(1024)S(1)}, f32[1024,768]{1,0:T(8,128)S(1)}, f32[768]{0:T(1024)}, f32[768]{0:T(1024)}) fusion(f32[1024]{0:T(1024)S(1)} %bitcast.236, f32[1024]{0:T(1024)S(1)} %bitcast.238, bf16[2,256,768]{2,1,0:T(8,128)(2,1)S(1)} %collective-permute-done.1, bf16[1,256,768]{2,1,0:T(8,128)(2,1)S(1)} %collective-permute-done, ...), kind=kOutput, calls=%fused_computation.181 | convolution fusion | flops 1218966528 | bytes 10643456 | tf_op jit(solution)/shard_map/dot_general | solution.py:91
  231.2 1.3 slice.302
  233.6 1.4 fusion.77
  237.0 4.4 convolution_convert_fusion
  241.4 1.8 convert_add_fusion
  244.7 1.2 slice.288
  247.1 1.9 convert_add_fusion.1
  249.1 2.1 collective-permute-start.8
  251.2 5.2 %collective-permute-done.12 = bf16[1,256,768]{2,1,0:T(8,128)(2,1)} collective-permute-done((bf16[1,256,768]{2,1,0:T(8,128)(2,1)}, bf16[1,256,768]{2,1,0:T(8,128)(2,1)}, u32[]{:S(2)}, u32[]{:S(2)}) %collective-permute-start.12) | collective-permute-done | bytes 393248 | tf_op jit(solution)/shard_map/ppermute | solution.py:26
  256.4 1.2 fusion.71
  257.9 6.0 %collective-permute-done.8 = bf16[1,256,768]{2,1,0:T(8,128)(2,1)S(1)} collective-permute-done((bf16[1,256,768]{2,1,0:T(8,128)(2,1)S(1)}, bf16[1,256,768]{2,1,0:T(8,128)(2,1)S(1)}, u32[]{:S(2)}, u32[]{:S(2)}) %collective-permute-start.8) | collective-permute-done | bytes 393248 | tf_op jit(solution)/shard_map/ppermute | solution.py:26
  264.0 1.3 convert_reduce_fusion.2
  267.0 3.5 collective-permute-done.13
  270.5 3.9 collective-permute-done.14
  274.5 4.5 collective-permute-done.15
  279.7 1.4 convert_element_type.205
  281.1 42.9 %reduce-scatter.5.cloned.1.call-done = bf16[96,576]{1,0:T(8,128)(2,1)} async-done(((bf16[768,576]{1,0:T(8,128)(2,1)}), bf16[96,576]{1,0:T(8,128)(2,1)}) %reduce-scatter.5.cloned.1.call-update) | async-done | bytes 110608 | tf_op jit(solution)/shard_map/reduce_scatter | solution.py:250
  324.0 3.3 all-to-all-start.3
  327.4 2.0 collective-permute-start.17
  329.4 2.4 all-to-all-done.3
  333.9 57.1 %reduce-scatter.9.cloned.1.call-done = bf16[96,768]{1,0:T(8,128)(2,1)} async-done(((bf16[768,768]{1,0:T(8,128)(2,1)}), bf16[96,768]{1,0:T(8,128)(2,1)}) %reduce-scatter.9.cloned.1.call-update) | async-done | bytes 147472 | tf_op jit(solution)/shard_map/reduce_scatter | solution.py:250
  391.0 3.3 all-to-all-start.5
  394.9 63.0 %reduce-scatter.11.cloned.1.call-done = bf16[96,768]{1,0:T(8,128)(2,1)} async-done(((bf16[768,768]{1,0:T(8,128)(2,1)}), bf16[96,768]{1,0:T(8,128)(2,1)}) %reduce-scatter.11.cloned.1.call-update) | async-done | bytes 147472 | tf_op jit(solution)/shard_map/reduce_scatter | solution.py:250
  457.9 1.6 convert_element_type.213
  (253 shorter events, 47.3 us)
Async XLA Ops:
  7.2 24.4 %copy-start = (s32[4]{0:T(128)S(1)}, s32[4]{0:T(128)}, u32[]{:S(2)}) copy-start(s32[4]{0:T(128)} %constant.65.clone) | copy-start | bytes 52
  7.2 25.6 %copy-start.1 = (s32[8]{0:T(128)S(1)}, s32[8]{0:T(128)}, u32[]{:S(2)}) copy-start(s32[8]{0:T(128)} %constant.66.clone) | copy-start | bytes 100
  7.2 24.2 %copy-start.3 = (bf16[2,128,768]{2,1,0:T(8,128)(2,1)S(1)}, bf16[2,128,768]{2,1,0:T(8,128)(2,1)}, u32[]{:S(2)}) copy-start(bf16[2,128,768]{2,1,0:T(8,128)(2,1)} %param.19) | copy-start | bytes 1179652
  7.2 26.3 %copy-start.22 = (bf16[24,768]{1,0:T(8,128)(2,1)S(1)}, bf16[24,768]{1,0:T(8,128)(2,1)}, u32[]{:S(2)}) copy-start(bf16[24,768]{1,0:T(8,128)(2,1)} %param.23) | copy-start | bytes 110596
  7.2 204.6 %all-gather.3.cloned.1.call-start = ((), (), s32[]{:S(2)}) async-start(), calls=%async_computation.10 | async-start | bytes 1327104 | tf_op jit(solution)/shard_map/all_gather | solution.py:156
  17.6 67.5 %collective-permute-start = (bf16[1,256,768]{2,1,0:T(8,128)(2,1)}, bf16[1,256,768]{2,1,0:T(8,128)(2,1)S(1)}, u32[]{:S(2)}, u32[]{:S(2)}) collective-permute-start(bf16[1,256,768]{2,1,0:T(8,128)(2,1)} %bitcast.196), channel_id=1, source_target_pairs={{0,2},{1,3},{2,0},{3,1},{4,6},{5,7},{6,4},{7,5},{8,10},{9,11},{10,... | collective-permute-start | bytes 1179656 | tf_op jit(solution)/shard_map/ppermute | solution.py:26
  23.5 47.1 %collective-permute-start.2 = (bf16[1,312]{1,0:T(2,128)(2,1)S(1)}, bf16[1,312]{1,0:T(2,128)(2,1)S(1)}, u32[]{:S(2)}, u32[]{:S(2)}) collective-permute-start(bf16[1,312]{1,0:T(2,128)(2,1)S(1)} %broadcast_in_dim.73), channel_id=1, source_target_pairs={{0,2},{1,3},{2,0},{3,1},{4,6},{5,7},{6,4},{7,5},{8,10},{9,11},{10,... | collective-permute-start | bytes 1880 | tf_op jit(solution)/shard_map/ppermute | solution.py:26
  25.2 104.1 %collective-permute-start.9 = (bf16[1,256,768]{2,1,0:T(8,128)(2,1)}, bf16[1,256,768]{2,1,0:T(8,128)(2,1)S(1)}, u32[]{:S(2)}, u32[]{:S(2)}) collective-permute-start(bf16[1,256,768]{2,1,0:T(8,128)(2,1)} %bitcast.210), channel_id=1, source_target_pairs={{0,2},{1,3},{2,0},{3,1},{4,6},{5,7},{6,4},{7,5},{8,10},{9,11},{10,... | collective-permute-start | bytes 1179656 | tf_op jit(solution)/shard_map/ppermute | solution.py:26
  27.3 61.3 %all-to-all-start = ((bf16[24,4,576]{2,0,1:T(8,128)(2,1)}), bf16[24,4,576]{2,0,1:T(8,128)(2,1)S(1)}, u32[]{:S(2)}, u32[]{:S(2)}) async-start(bf16[24,4,576]{2,0,1:T(8,128)(2,1)} %copy.80), calls=%async_computation | async-start | bytes 245760 | tf_op jit(solution)/shard_map/all_to_all | solution.py:155
  30.7 185.6 %all-gather.5.cloned.1.call-start = ((), (), s32[]{:S(2)}) async-start(), calls=%async_computation.11 | async-start | bytes 1327104 | tf_op jit(solution)/shard_map/all_gather | solution.py:157
  69.0 15.5 %copy-start.28 = (f32[2,128]{1,0:T(2,128)}, f32[2,128]{1,0:T(2,128)S(1)}, u32[]{:S(2)}) copy-start(f32[2,128]{1,0:T(2,128)S(1)} %get-tuple-element.62) | copy-start | bytes 3076
  69.2 60.1 %copy-start.6 = (bf16[2,128,768]{2,1,0:T(8,128)(2,1)S(1)}, bf16[2,128,768]{2,1,0:T(8,128)(2,1)}, u32[]{:S(2)}) copy-start(bf16[2,128,768]{2,1,0:T(8,128)(2,1)} %param.20) | copy-start | bytes 1179652
  70.6 1.2 collective-permute-start.3
  72.4 4.6 collective-permute-start.4
  77.0 3.7 collective-permute-start.5
  80.7 3.8 collective-permute-start.6
  85.2 45.1 %collective-permute-start.1 = (bf16[2,256,768]{2,1,0:T(8,128)(2,1)S(1)}, bf16[2,256,768]{2,1,0:T(8,128)(2,1)S(1)}, u32[]{:S(2)}, u32[]{:S(2)}) collective-permute-start(bf16[2,256,768]{2,1,0:T(8,128)(2,1)S(1)} %pad_maximum_fusion.3), channel_id=1, source_target_pairs={{0,1},{1,0},{2,3},{3,2},{4,5},{5,4},{6,7},{7,6},{8,9},{9,8},{10,11... | collective-permute-start | bytes 2359304 | tf_op jit(solution)/shard_map/ppermute | solution.py:26
  89.3 39.3 %all-to-all-start.1 = ((bf16[4,48,768]{2,1,0:T(8,128)(2,1)}), bf16[4,48,768]{2,1,0:T(8,128)(2,1)S(1)}, u32[]{:S(2)}, u32[]{:S(2)}) async-start(bf16[4,48,768]{2,1,0:T(8,128)(2,1)} %bitcast.21), calls=%async_computation.1 | async-start | bytes 589824 | tf_op jit(solution)/shard_map/all_to_all | solution.py:160
  130.3 17.6 %collective-permute-start.10 = (bf16[2,256,768]{2,1,0:T(8,128)(2,1)}, bf16[2,256,768]{2,1,0:T(8,128)(2,1)}, u32[]{:S(2)}, u32[]{:S(2)}) collective-permute-start(bf16[2,256,768]{2,1,0:T(8,128)(2,1)} %pad_maximum_fusion.4), channel_id=1, source_target_pairs={{0,1},{1,0},{2,3},{3,2},{4,5},{5,4},{6,7},{7,6},{8,9},{9,8},{10,11... | collective-permute-start | bytes 2359304 | tf_op jit(solution)/shard_map/ppermute | solution.py:26
  133.2 1.2 copy-start.16
  144.9 1.6 copy-start.10
  145.8 4.7 copy-start.14
  162.0 4.6 copy-start.2
  185.0 8.0 %copy-start.8 = (bf16[1024,192]{0,1:T(8,128)(2,1)}, bf16[1024,192]{0,1:T(8,128)(2,1)S(1)}, u32[]{:S(2)}) copy-start(bf16[1024,192]{0,1:T(8,128)(2,1)S(1)} %reshape.592) | copy-start | bytes 1179652
  187.8 10.4 %all-to-all-start.4 = ((bf16[4,48,768]{2,1,0:T(8,128)(2,1)}), bf16[4,48,768]{2,1,0:T(8,128)(2,1)S(1)}, u32[]{:S(2)}, u32[]{:S(2)}) async-start(bf16[4,48,768]{2,1,0:T(8,128)(2,1)} %bitcast.222), calls=%async_computation.5 | async-start | bytes 589824 | tf_op jit(solution)/shard_map/all_to_all | solution.py:260
  191.4 88.3 %reduce-scatter.7.cloned.1.call-start = ((), (), s32[]{:S(2)}) async-start(), calls=%async_computation.13 | async-start | bytes 331776 | tf_op jit(solution)/shard_map/reduce_scatter | solution.py:250
  198.9 125.2 %reduce-scatter.5.cloned.1.call-start = ((), (), s32[]{:S(2)}) async-start(), calls=%async_computation.12 | async-start | bytes 1105920 | tf_op jit(solution)/shard_map/reduce_scatter | solution.py:250
  203.1 6.1 %copy-start.26 = (f32[1,2,4,128]{3,2,1,0:T(4,128)S(1)}, f32[1,2,4,128]{3,2,1,0:T(4,128)}, u32[]{:S(2)}) copy-start(f32[1,2,4,128]{3,2,1,0:T(4,128)} %get-tuple-element.51) | copy-start | bytes 12292
  203.1 6.1 %copy-start.25 = (f32[1,2,4,128]{3,2,1,0:T(4,128)S(1)}, f32[1,2,4,128]{3,2,1,0:T(4,128)}, u32[]{:S(2)}) copy-start(f32[1,2,4,128]{3,2,1,0:T(4,128)} %get-tuple-element.52) | copy-start | bytes 12292
  203.1 7.2 %copy-start.23 = (f32[768]{0:T(1024)S(1)}, f32[768]{0:T(1024)}, u32[]{:S(2)}) copy-start(f32[768]{0:T(1024)} %mul.264) | copy-start | bytes 9220
  203.1 7.2 %copy-start.24 = (f32[768]{0:T(1024)S(1)}, f32[768]{0:T(1024)}, u32[]{:S(2)}) copy-start(f32[768]{0:T(1024)} %add.267) | copy-start | bytes 9220
  207.8 4.1 copy-start.31
  207.8 183.2 %reduce-scatter.9.cloned.1.call-start = ((), (), s32[]{:S(2)}) async-start(), calls=%async_computation.14 | async-start | bytes 1327104 | tf_op jit(solution)/shard_map/reduce_scatter | solution.py:250
  225.4 232.5 %reduce-scatter.11.cloned.1.call-start = ((), (), s32[]{:S(2)}) async-start(), calls=%async_computation.15 | async-start | bytes 1327104 | tf_op jit(solution)/shard_map/reduce_scatter | solution.py:250
  231.2 2.2 copy-start.39
  231.2 2.4 copy-start.40
  233.4 8.0 %collective-permute-start.11 = (bf16[2,256,768]{2,1,0:T(8,128)(2,1)}, bf16[2,256,768]{2,1,0:T(8,128)(2,1)}, u32[]{:S(2)}, u32[]{:S(2)}) collective-permute-start(bf16[2,256,768]{2,1,0:T(8,128)(2,1)} %bitcast.44), channel_id=1, source_target_pairs={{0,1},{1,0},{2,3},{3,2},{4,5},{5,4},{6,7},{7,6},{8,9},{9,8},{10,11... | collective-permute-start | bytes 2359304 | tf_op jit(solution)/shard_map/ppermute | solution.py:26
  233.6 1.4 copy-start.9
  233.6 1.4 copy-start.15
  235.0 2.0 copy-start.32
  236.6 10.4 %collective-permute-start.7 = (bf16[2,256,768]{2,1,0:T(8,128)(2,1)}, bf16[2,256,768]{2,1,0:T(8,128)(2,1)}, u32[]{:S(2)}, u32[]{:S(2)}) collective-permute-start(bf16[2,256,768]{2,1,0:T(8,128)(2,1)} %bitcast.30), channel_id=1, source_target_pairs={{0,1},{1,0},{2,3},{3,2},{4,5},{5,4},{6,7},{7,6},{8,9},{9,8},{10,11... | collective-permute-start | bytes 2359304 | tf_op jit(solution)/shard_map/ppermute | solution.py:26
  241.4 2.6 copy-start.38
  243.2 2.8 copy-start.4
  243.2 3.5 copy-start.30
  244.1 12.3 %collective-permute-start.12 = (bf16[1,256,768]{2,1,0:T(8,128)(2,1)}, bf16[1,256,768]{2,1,0:T(8,128)(2,1)}, u32[]{:S(2)}, u32[]{:S(2)}) collective-permute-start(bf16[1,256,768]{2,1,0:T(8,128)(2,1)} %slice.369), channel_id=1, source_target_pairs={{0,2},{1,3},{2,0},{3,1},{4,6},{5,7},{6,4},{7,5},{8,10},{9,11},{10,... | collective-permute-start | bytes 1179656 | tf_op jit(solution)/shard_map/ppermute | solution.py:26
  247.1 9.3 %copy-start.5 = (f32[2,256,768]{2,1,0:T(8,128)S(1)}, f32[2,256,768]{2,1,0:T(8,128)}, u32[]{:S(2)}) copy-start(f32[2,256,768]{2,1,0:T(8,128)} %copy-done.4) | copy-start | bytes 4718596
  249.0 8.6 %copy-start.33 = (f32[256]{0:T(256)S(1)}, f32[256]{0:T(256)}, u32[]{:S(2)}) copy-start(f32[256]{0:T(256)} %get-tuple-element.61) | copy-start | bytes 3076
  249.0 8.6 %copy-start.34 = (f32[256]{0:T(256)S(1)}, f32[256]{0:T(256)}, u32[]{:S(2)}) copy-start(f32[256]{0:T(256)} %get-tuple-element.60) | copy-start | bytes 3076
  249.0 14.9 %copy-start.7 = (bf16[2,128,768]{2,1,0:T(8,128)(2,1)S(1)}, bf16[2,128,768]{2,1,0:T(8,128)(2,1)}, u32[]{:S(2)}) copy-start(bf16[2,128,768]{2,1,0:T(8,128)(2,1)} %param.20) | copy-start | bytes 1179652
  249.0 14.9 %copy-start.27 = (f32[768]{0:T(1024)S(1)}, f32[768]{0:T(1024)}, u32[]{:S(2)}) copy-start(f32[768]{0:T(1024)} %add.281) | copy-start | bytes 9220
  249.1 14.9 %copy-start.29 = (f32[2,128]{1,0:T(2,128)S(1)}, f32[2,128]{1,0:T(2,128)}, u32[]{:S(2)}) copy-start(f32[2,128]{1,0:T(2,128)} %copy-done.28) | copy-start | bytes 3076
  249.1 14.9 %copy-start.35 = (f32[2,128]{1,0:T(2,128)S(1)}, f32[2,128]{1,0:T(2,128)}, u32[]{:S(2)}) copy-start(f32[2,128]{1,0:T(2,128)} %get-tuple-element.59) | copy-start | bytes 3076
  249.1 14.8 %collective-permute-start.8 = (bf16[1,256,768]{2,1,0:T(8,128)(2,1)S(1)}, bf16[1,256,768]{2,1,0:T(8,128)(2,1)S(1)}, u32[]{:S(2)}, u32[]{:S(2)}) collective-permute-start(bf16[1,256,768]{2,1,0:T(8,128)(2,1)S(1)} %slice.370), channel_id=1, source_target_pairs={{0,2},{1,3},{2,0},{3,1},{4,6},{5,7},{6,4},{7,5},{8,10},{9,11},{10,... | collective-permute-start | bytes 1179656 | tf_op jit(solution)/shard_map/ppermute | solution.py:26
  257.9 7.6 %copy-start.20 = (f32[8,4,72]{2,1,0:T(4,128)S(1)}, f32[8,4,72]{2,1,0:T(4,128)}, u32[]{:S(2)}) copy-start(f32[8,4,72]{2,1,0:T(4,128)} %reshape.600) | copy-start | bytes 27652
  257.9 7.6 %copy-start.21 = (f32[8,4,96]{2,1,0:T(4,128)S(1)}, f32[8,4,96]{2,1,0:T(4,128)}, u32[]{:S(2)}) copy-start(f32[8,4,96]{2,1,0:T(4,128)} %broadcast_select_fusion) | copy-start | bytes 36868
  264.0 10.6 %copy-start.36 = (s32[4]{0:T(128)S(1)}, s32[4]{0:T(128)}, u32[]{:S(2)}) copy-start(s32[4]{0:T(128)} %get-tuple-element.63) | copy-start | bytes 52
  266.3 4.1 collective-permute-start.13
  270.4 3.9 collective-permute-start.14
  274.4 4.6 collective-permute-start.15
  279.6 47.8 %collective-permute-start.16 = (f32[2,288]{1,0:T(2,128)S(1)}, f32[2,288]{1,0:T(2,128)S(1)}, u32[]{:S(2)}, u32[]{:S(2)}) collective-permute-start(f32[2,288]{1,0:T(2,128)S(1)} %slice.313), channel_id=1, source_target_pairs={{0,1},{1,0},{2,3},{3,2},{4,5},{5,4},{6,7},{7,6},{8,9},{9,8},{10,11... | collective-permute-start | bytes 6920 | tf_op jit(solution)/shard_map/ppermute | solution.py:26
  324.0 7.8 %all-to-all-start.3 = ((bf16[4,24,576]{2,1,0:T(8,128)(2,1)}), bf16[4,24,576]{2,1,0:T(8,128)(2,1)S(1)}, u32[]{:S(2)}, u32[]{:S(2)}) async-start(bf16[4,24,576]{2,1,0:T(8,128)(2,1)} %bitcast.229), calls=%async_computation.4 | async-start | bytes 245760 | tf_op jit(solution)/shard_map/all_to_all | solution.py:257
  327.4 5.4 %collective-permute-start.17 = (f32[1,288]{1,0:T(1,128)S(1)}, f32[1,288]{1,0:T(1,128)S(1)}, u32[]{:S(2)}, u32[]{:S(2)}) collective-permute-start(f32[1,288]{1,0:T(1,128)S(1)} %slice.315), channel_id=1, source_target_pairs={{0,2},{1,3},{2,0},{3,1},{4,6},{5,7},{6,4},{7,5},{8,10},{9,11},{10,... | collective-permute-start | bytes 3464 | tf_op jit(solution)/shard_map/ppermute | solution.py:26
  333.9 127.7 %copy-start.37 = (f32[24]{0:T(128)}, f32[24]{0:T(128)S(1)}, u32[]{:S(2)}) copy-start(f32[24]{0:T(128)S(1)} %get-tuple-element.99) | copy-start | bytes 292
  391.0 68.6 %all-to-all-start.5 = ((bf16[4,24,768]{2,1,0:T(8,128)(2,1)}), bf16[4,24,768]{2,1,0:T(8,128)(2,1)S(1)}, u32[]{:S(2)}, u32[]{:S(2)}) async-start(bf16[4,24,768]{2,1,0:T(8,128)(2,1)} %bitcast.228), calls=%async_computation.8 | async-start | bytes 294912 | tf_op jit(solution)/shard_map/all_to_all | solution.py:253
  (7 other events, 6.1 us)
Sparse Core Ops, SparseCore 0:
  17.7 43.2 all-gather.2
  63.3 41.3 all-gather.4
  199.0 58.5 reduce-scatter.6
  260.7 63.2 reduce-scatter.4
  327.3 63.7 reduce-scatter.8
  394.3 63.6 reduce-scatter.10
